TPU v7x, 32 devices: a whole 2x2x4 slice. The times are simulated.
32 devices in a mesh: side: 4 (over y, x), edge: 8 (over z, core).
Axes of the slice: x: 2, y: 2, z: 4, core: 2. Of those that a mesh axis runs over, the one named last changes fastest.
Arguments:
- parent_blocks: bfloat16 [32, 450, 128], P(('side', 'edge')), may hold values from -6 to 6
- interp_weight: bfloat16 [128, 2, 128, 128], P(('side', 'edge')), may hold values from -0.375 to 0.375
- tile_source: int32 [128, 2], P(('side', 'edge')), may hold values from 0 to 31, as said below
- destination: int32 [16384, 1], P(('side', 'edge')), may hold values from 0 to 7; in each aligned block of 512 rows (0 to 511, 512 to 1023, ...) at most 128 rows name the same one
- remap_matrix: bfloat16 [5, 400, 90], replicated, may hold values from -0.625 to 0.625
Outputs:
- forcing: bfloat16 [5, 400, 32768], P(None, None, ('side', 'edge'))
Inputs may be any that keep to these rules, and one draw needn't show every extreme that they name: `tile_source`: the two blocks of a tile are distinct, and each is the tile's own device d or d - 1 or d + 1 modulo 32 along the loop of devices. `destination`: among the rows of one device no owner is named more than 128 times, and in some devices some owner is named exactly 128 times.
All inputs are finite; a program needn't handle non-finite values.
Results may differ from a plain program's by a relative error of at most 0.0049.
Values may be sent and summed in bfloat16 or wider, within the bound.
No kernel may reach another device: no remote copies, remote signals or barrier semaphores. Data moves between devices by JAX's collectives and lax.ppermute only.
A program may use at most 64 MiB of HBM per device.

v0:
```python
import jax
import jax.numpy as jnp
from jax import lax
from jax.sharding import PartitionSpec as P


def padded(array, sides, width):
    for axis, dim in sides:
        devices, length = (lax.axis_size(axis), array.shape[dim])
        up = [(i, (i + 1) % devices) for i in range(devices)]
        down = [(j, i) for i, j in up]
        last = lax.slice_in_dim(array, length - width, length, axis=dim)
        leading = lax.slice_in_dim(array, 0, width, axis=dim)
        before = lax.ppermute(last, axis, up)
        after = lax.ppermute(leading, axis, down)
        array = jnp.concatenate([before, array, after], axis=dim)
    return array


def remap_rows(remap_matrix, rows):
    shaped = rows.reshape(remap_matrix.shape[0], remap_matrix.shape[2], rows.shape[1])
    result = jnp.einsum("vcl,vln->vcn", remap_matrix, shaped, preferred_element_type=jnp.float32)
    return result.astype(jnp.bfloat16)


def body(parent_blocks, interp_weight, tile_source, destination, remap_matrix):
    edge_count = lax.axis_size("edge")
    block_count = lax.axis_size("side") * edge_count
    position = lax.axis_index("side") * edge_count + lax.axis_index("edge")
    rim_blocks = padded(parent_blocks, ((("side", "edge"), 0),), 1)
    offset = (tile_source - position + 1 + block_count) % block_count
    chosen = rim_blocks[offset]
    summed = jnp.einsum("tkfp,tkpr->tfr", chosen, interp_weight, preferred_element_type=jnp.float32)
    coarse = summed.astype(jnp.bfloat16)
    tile_count, feat_count, tile_rows = coarse.shape
    rows = coarse.transpose(1, 0, 2).reshape(feat_count, tile_count * tile_rows)
    row_count = destination.shape[0]
    capacity = max(2, 2 * row_count // edge_count)
    owners = destination[:, 0]
    owner_hits = (owners[:, None] == jnp.arange(edge_count, dtype=jnp.int32)[None, :]).astype(
        jnp.int32
    )
    places = jnp.sum(jnp.cumsum(owner_hits, axis=0) * owner_hits, axis=1) - 1
    slot_index = owners * capacity + places
    outbox = (
        jnp.zeros((feat_count, edge_count * capacity), jnp.bfloat16).at[:, slot_index].set(rows)
    )
    inbox = lax.all_to_all(outbox, "edge", split_axis=1, concat_axis=1, tiled=True)
    forcing = remap_rows(remap_matrix, inbox)
    return forcing


def solution(mesh):
    return jax.shard_map(
        body,
        mesh=mesh,
        in_specs=(
            P(("side", "edge"), None, None),
            P(("side", "edge"), None, None, None),
            P(("side", "edge"), None),
            P(("side", "edge"), None),
            P(),
        ),
        out_specs=P(None, None, ("side", "edge")),
        check_vma=False,
    )
```

profile of v0, /device:TPU:0, one launch (start us, length us, event | category | flops | bytes accessed | tf_op | source)
XLA Modules:
  0.0 49.2 jit_solution(1207886696506333563)
XLA Ops:
  0.0 0.0 copy-start
  0.0 0.5 collective-permute-start
  0.5 6.0 %collective-permute-start.1 = (bf16[1,450,128]{2,1,0:T(8,128)(2,1)}, bf16[1,450,128]{2,1,0:T(8,128)(2,1)S(1)}, u32[]{:S(2)}, u32[]{:S(2)}) collective-permute-start(bf16[1,450,128]{2,1,0:T(8,128)(2,1)} %param.5), channel_id=1, source_target_pairs={{1,0},{2,1},{3,2},{4,3},{5,4},{6,5},{7,6},{8,7},{9,8},{10,9},{11,1... | collective-permute-start | bytes 345608 | tf_op jit(solution)/shard_map/ppermute | solution.py:15
  6.4 0.7 %fusion.5 = s32[8,4,128]{2,0,1:T(8,128)S(1)} fusion(s32[4,128]{1,0:T(4,128)} %bitcast.37), kind=kLoop, calls=%fused_computation.14 | loop fusion | flops 8192 | bytes 18432 | tf_op jit(solution)/shard_map/convert_element_type | solution.py:40
  7.1 1.1 %reduce-window.6 = s32[8,4,128]{2,0,1:T(8,128)S(1)} reduce-window(s32[8,4,128]{2,0,1:T(8,128)S(1)} %fusion.5, s32[]{:T(128)} %constant.21.clone.1), window={size=1x1x128 pad=0_0x0_0x127_0}, to_apply=%region_0.1 | reduce-window | flops 520192 | bytes 32772 | tf_op jit(solution)/shard_map/reduce-window
  8.2 0.2 slice_reduce_fusion
  8.5 0.8 %fusion.4 = s32[512]{0:T(512)S(1)} fusion(s32[8,4,128]{2,0,1:T(8,128)S(1)} %reduce-window.6, s32[8,4]{0,1:T(4,128)S(1)} %slice.7, s32[512]{0:T(512)} %bitcast.38), kind=kLoop, calls=%fused_computation.11 | loop fusion | flops 15872 | bytes 20608 | tf_op jit(solution)/shard_map/reduce_sum | solution.py:43
  9.3 0.7 %compare_select_fusion = s32[512,1]{0,1:T(1,128)S(1)} fusion(s32[512,1]{0,1:T(1,128)S(1)} %bitcast.39, s32[512,1]{0,1:T(1,128)} %param.8), kind=kLoop, calls=%fused_computation.15 | loop fusion | flops 2560 | bytes 6144 | tf_op jit(solution)/shard_map/select_n | solution.py:46
  10.0 0.7 %compare_select_fusion.1 = s32[4,2]{0,1:T(2,128)S(1)} fusion(s32[4,2]{0,1:T(2,128)} %param.7, s32[]{:T(128)S(6)} %add.43), kind=kLoop, calls=%fused_computation.17 | loop fusion | flops 128 | bytes 68 | tf_op jit(solution)/shard_map/select_n | solution.py:32
  10.7 0.1 copy.12
  10.8 0.1 reshape.39
  10.9 0.0 collective-permute-done
  10.9 0.0 collective-permute-done.1
  10.9 0.9 %pad_maximum_fusion = bf16[3,450,128]{2,1,0:T(8,128)(2,1)S(1)} fusion(bf16[1,450,128]{2,1,0:T(8,128)(2,1)S(1)} %collective-permute-done.1, bf16[1,450,128]{2,1,0:T(8,128)(2,1)} %param.5, bf16[1,450,128]{2,1,0:T(8,128)(2,1)S(1)} %collective-permute-done), kind=kLoop, calls=%fused_computation.8 | loop fusion | flops 345600 | bytes 691200 | tf_op jit(solution)/shard_map/concatenate | solution.py:16
  11.8 0.7 %gather_fusion = bf16[8,450,128]{2,1,0:T(8,128)(2,1)S(1)} fusion(bf16[3,450,128]{2,1,0:T(8,128)(2,1)S(1)} %pad_maximum_fusion, s32[1024]{0:T(1024)S(1)} %pad_clamp_fusion), kind=kCustom, calls=%fused_computation | custom fusion | bytes 1843232 | tf_op jit(solution)/shard_map/gather | solution.py:32
  12.5 1.4 %fusion.1 = bf16[450,4,128]{2,0,1:T(8,128)(2,1)S(1)} fusion(bf16[4,2,450,128]{3,2,1,0:T(8,128)(2,1)S(1)} %bitcast.34, bf16[4,2,128,128]{3,2,1,0:T(8,128)(2,1)} %param.6), kind=kOutput, calls=%fused_computation.5 | convolution fusion | flops 118195200 | bytes 1644544 | tf_op jit(solution)/shard_map/tkfp,tkpr->tfr/dot_general | solution.py:33
  13.9 0.2 copy.13
  14.1 0.2 pad.4
  14.3 0.1 copy.18
  14.4 0.2 copy.14
  14.6 2.7 %scatter_custom_fusion = bf16[450,1024]{0,1:T(8,128)(2,1)S(1)} fusion(s32[512]{0:T(512)S(1)} %bitcast.40, bf16[512,450]{1,0:T(8,128)(2,1)S(1)} %copy.14, bf16[]{:T(256)} %constant.16.clone.1), kind=kCustom, calls=%fused_computation.6 | custom fusion | bytes 921602 | tf_op jit(solution)/shard_map/scatter | solution.py:46
  17.3 0.6 %copy.15 = bf16[450,8,128]{2,0,1:T(8,128)(2,1)S(1)} copy(bf16[450,8,128]{0,2,1:T(8,128)(2,1)S(1)} %bitcast.33) | data formatting | bytes 1843200 | tf_op jit(solution)/shard_map/all_to_all | solution.py:48
  18.0 27.4 %all_to_all.9 = bf16[450,8,128]{2,0,1:T(8,128)(2,1)S(1)} all-to-all(bf16[450,8,128]{2,0,1:T(8,128)(2,1)S(1)} %copy.15), channel_id=1, replica_groups=mesh['side'=4,'edge'=8] {'edge'}, dimensions={1} | all-to-all | bytes 1843200 | tf_op jit(solution)/shard_map/all_to_all | solution.py:48
  45.4 0.1 copy.16
  45.5 0.4 reshape.36
  45.9 0.0 copy-done
  45.9 3.2 %convert_bitcast_fusion = bf16[5,400,1024]{2,1,0:T(8,128)(2,1)} fusion(bf16[5,90,1024]{2,1,0:T(8,128)(2,1)S(1)} %reshape.36, bf16[5,400,90]{1,2,0:T(8,128)(2,1)S(1)} %copy-done), kind=kOutput, calls=%fused_computation.2 | convolution fusion | flops 370688000 | bytes 5377600 | tf_op jit(solution)/shard_map/vcl,vln->vcn/dot_general | solution.py:22
  (4 shorter events, 0.1 us)
Async XLA Ops:
  0.0 45.9 %copy-start = (bf16[5,400,90]{1,2,0:T(8,128)(2,1)S(1)}, bf16[5,400,90]{1,2,0:T(8,128)(2,1)}, u32[]{:S(2)}) copy-start(bf16[5,400,90]{1,2,0:T(8,128)(2,1)} %param.9) | copy-start | bytes 1080004
  0.0 10.9 %collective-permute-start = (bf16[1,450,128]{2,1,0:T(8,128)(2,1)}, bf16[1,450,128]{2,1,0:T(8,128)(2,1)S(1)}, u32[]{:S(2)}, u32[]{:S(2)}) collective-permute-start(bf16[1,450,128]{2,1,0:T(8,128)(2,1)} %param.5), channel_id=1, source_target_pairs={{0,1},{1,2},{2,3},{3,4},{4,5},{5,6},{6,7},{7,8},{8,9},{9,10},{10,1... | collective-permute-start | bytes 345608 | tf_op jit(solution)/shard_map/ppermute | solution.py:14
  0.5 10.4 %collective-permute-start.1 = (bf16[1,450,128]{2,1,0:T(8,128)(2,1)}, bf16[1,450,128]{2,1,0:T(8,128)(2,1)S(1)}, u32[]{:S(2)}, u32[]{:S(2)}) collective-permute-start(bf16[1,450,128]{2,1,0:T(8,128)(2,1)} %param.5), channel_id=1, source_target_pairs={{1,0},{2,1},{3,2},{4,3},{5,4},{6,5},{7,6},{8,7},{9,8},{10,9},{11,1... | collective-permute-start | bytes 345608 | tf_op jit(solution)/shard_map/ppermute | solution.py:15
where the time goes:
time: 49.4 us; the launch traced here: 49.2 us
  blocking collectives  27.4 us (55%)
  starting transfers between devices  6.43 us (13%)
  local copies, waits for them, and re-layouts  5.66 us (11%)
  other arithmetic  4.95 us (10%)
  matrix products  4.61 us (9%)
    all_to_all x1, blocking collectives, body(): lax.all_to_all(outbox, 'edge', split_axis=1, concat_axis=1, tiled=True)  27.4 us
    ppermute x1, starting transfers between devices, padded(): after = lax.ppermute(leading, axis, down)  5.98 us
    dot_general x1, matrix products, remap_rows(): jnp.einsum('vcl,vln->vcn', remap_matrix, shaped, preferred_element_type=j...  3.24 us
    scatter x1, local copies, waits for them, and re-layouts, body(): jnp.zeros((feat_count, edge_count * capacity), jnp.bfloat16)  2.74 us
    dot_general x1, matrix products, body(): jnp.einsum('tkfp,tkpr->tfr', chosen, interp_weight, preferred_element_typ...  1.36 us
    another operation x2, other arithmetic  1.16 us
  transfers between devices with their start and end apart: 2, of which 0 were waited for; matrix products, arithmetic and copies ran while one was open for 9% of the time, Pallas kernels for 0%

commit v1 on v0

--- a/solution.py
+++ b/solution.py
@@ -2,6 +2,17 @@
 import jax.numpy as jnp
 from jax import lax
 from jax.sharding import PartitionSpec as P
+
+
+def split_up(array, dim, size):
+    before, after = (array.shape[:dim], array.shape[dim + 1 :])
+    return jnp.moveaxis(array.reshape(*before, size, -1, *after), dim, 0)
+
+
+def laid_out(blocks, dim):
+    blocks = jnp.moveaxis(blocks, 0, dim)
+    lengths = blocks.shape
+    return blocks.reshape(*lengths[:dim], lengths[dim] * lengths[dim + 1], *lengths[dim + 2 :])
 
 
 def padded(array, sides, width):
@@ -45,7 +56,14 @@
     outbox = (
         jnp.zeros((feat_count, edge_count * capacity), jnp.bfloat16).at[:, slot_index].set(rows)
     )
-    inbox = lax.all_to_all(outbox, "edge", split_axis=1, concat_axis=1, tiled=True)
+    peers, index = (lax.axis_size("edge"), lax.axis_index("edge"))
+    blocks = split_up(outbox, 1, peers)
+    gathered = [blocks[index]]
+    for step in range(1, peers):
+        sent = blocks[index ^ step]
+        gathered.append(lax.ppermute(sent, "edge", [(i_2, i_2 ^ step) for i_2 in range(peers)]))
+    blocks = jnp.stack(gathered)[index ^ jnp.arange(peers)]
+    inbox = laid_out(blocks, 1)
     forcing = remap_rows(remap_matrix, inbox)
     return forcing
 

time: 49.4 us -> 47.7 us (0.966)
  the two profiles are of different devices: /device:TPU:0 before, /device:TPU:19 now
where the time goes in v1:
time: 47.7 us; the launch traced here: 47.4 us
  waiting for transfers between devices  19.2 us (40%)
  starting transfers between devices  11.3 us (24%)
  local copies, waits for them, and re-layouts  7.15 us (15%)
  other arithmetic  4.96 us (10%)
  matrix products  4.61 us (10%)
    ppermute x7, waiting for transfers between devices, body(): lax.ppermute(sent, 'edge', [(i_2, i_2 ^ step) for i_2 in range(peers)])  19.2 us
    ppermute x7, starting transfers between devices, body(): lax.ppermute(sent, 'edge', [(i_2, i_2 ^ step) for i_2 in range(peers)])  9.4 us
    dot_general x1, matrix products, remap_rows(): jnp.einsum('vcl,vln->vcn', remap_matrix, shaped, preferred_element_type=j...  3.24 us
    scatter x1, local copies, waits for them, and re-layouts, body(): jnp.zeros((feat_count, edge_count * capacity), jnp.bfloat16)  2.74 us
    ppermute x1, starting transfers between devices, padded(): before = lax.ppermute(last, axis, up)  1.86 us
    dot_general x1, matrix products, body(): jnp.einsum('tkfp,tkpr->tfr', chosen, interp_weight, preferred_element_typ...  1.36 us
    another operation x10, local copies, waits for them, and re-layouts  1.26 us
    another operation x2, other arithmetic  1.16 us
  transfers between devices with their start and end apart: 9, of which 5 were waited for; matrix products, arithmetic and copies ran while one was open for 10% of the time, Pallas kernels for 0%

profile of v1, /device:TPU:19, one launch (start us, length us, event | category | flops | bytes accessed | tf_op | source)
XLA Modules:
  0.0 47.4 jit_solution(12308929285116317781)
XLA Ops:
  0.0 0.0 copy-start
  0.0 1.9 %collective-permute-start = (bf16[1,450,128]{2,1,0:T(8,128)(2,1)}, bf16[1,450,128]{2,1,0:T(8,128)(2,1)S(1)}, u32[]{:S(2)}, u32[]{:S(2)}) collective-permute-start(bf16[1,450,128]{2,1,0:T(8,128)(2,1)} %param.5), channel_id=1, source_target_pairs={{0,1},{1,2},{2,3},{3,4},{4,5},{5,6},{6,7},{7,8},{8,9},{9,10},{10,1... | collective-permute-start | bytes 345608 | tf_op jit(solution)/shard_map/ppermute | solution.py:25
  1.9 0.0 collective-permute-start.1
  1.9 0.7 %compare_select_fusion.1 = s32[4,2]{0,1:T(2,128)S(1)} fusion(s32[4,2]{0,1:T(2,128)} %param.7, s32[]{:T(128)S(6)} %add.77), kind=kLoop, calls=%fused_computation.27 | loop fusion | flops 128 | bytes 68 | tf_op jit(solution)/shard_map/select_n | solution.py:43
  2.6 0.1 copy.18
  2.7 0.1 reshape.67
  2.7 0.7 %fusion.5 = s32[8,4,128]{2,0,1:T(8,128)S(1)} fusion(s32[4,128]{1,0:T(4,128)} %bitcast.71), kind=kLoop, calls=%fused_computation.23 | loop fusion | flops 8192 | bytes 18432 | tf_op jit(solution)/shard_map/convert_element_type | solution.py:51
  3.4 1.1 %reduce-window.6 = s32[8,4,128]{2,0,1:T(8,128)S(1)} reduce-window(s32[8,4,128]{2,0,1:T(8,128)S(1)} %fusion.5, s32[]{:T(128)} %constant.20.clone.1), window={size=1x1x128 pad=0_0x0_0x127_0}, to_apply=%region_0.1 | reduce-window | flops 520192 | bytes 32772 | tf_op jit(solution)/shard_map/reduce-window
  4.6 0.2 slice_reduce_fusion
  4.8 0.8 %fusion.4 = s32[512]{0:T(512)S(1)} fusion(s32[8,4,128]{2,0,1:T(8,128)S(1)} %reduce-window.6, s32[8,4]{0,1:T(4,128)S(1)} %slice.7, s32[512]{0:T(512)} %bitcast.72), kind=kLoop, calls=%fused_computation.20 | loop fusion | flops 15872 | bytes 20608 | tf_op jit(solution)/shard_map/reduce_sum | solution.py:54
  5.6 0.7 %compare_select_fusion = s32[512,1]{0,1:T(1,128)S(1)} fusion(s32[512,1]{0,1:T(1,128)S(1)} %bitcast.73, s32[512,1]{0,1:T(1,128)} %param.8), kind=kLoop, calls=%fused_computation.24 | loop fusion | flops 2560 | bytes 6144 | tf_op jit(solution)/shard_map/select_n | solution.py:57
  6.3 0.0 collective-permute-done
  6.4 0.0 collective-permute-done.1
  6.4 0.9 %pad_maximum_fusion = bf16[3,450,128]{2,1,0:T(8,128)(2,1)S(1)} fusion(bf16[1,450,128]{2,1,0:T(8,128)(2,1)S(1)} %collective-permute-done.1, bf16[1,450,128]{2,1,0:T(8,128)(2,1)} %param.5, bf16[1,450,128]{2,1,0:T(8,128)(2,1)S(1)} %collective-permute-done), kind=kLoop, calls=%fused_computation.9 | loop fusion | flops 345600 | bytes 691200 | tf_op jit(solution)/shard_map/concatenate | solution.py:27
  7.3 0.7 %gather_fusion = bf16[8,450,128]{2,1,0:T(8,128)(2,1)S(1)} fusion(bf16[3,450,128]{2,1,0:T(8,128)(2,1)S(1)} %pad_maximum_fusion, s32[1024]{0:T(1024)S(1)} %pad_clamp_fusion.1), kind=kCustom, calls=%fused_computation | custom fusion | bytes 1843232 | tf_op jit(solution)/shard_map/gather | solution.py:43
  8.1 1.4 %fusion.1 = bf16[450,4,128]{2,0,1:T(8,128)(2,1)S(1)} fusion(bf16[4,2,450,128]{3,2,1,0:T(8,128)(2,1)S(1)} %bitcast.60, bf16[4,2,128,128]{3,2,1,0:T(8,128)(2,1)} %param.6), kind=kOutput, calls=%fused_computation.6 | convolution fusion | flops 118195200 | bytes 1644544 | tf_op jit(solution)/shard_map/tkfp,tkpr->tfr/dot_general | solution.py:44
  9.4 0.2 copy.19
  9.6 0.2 pad.5
  9.8 0.1 copy.31
  9.9 0.2 copy.20
  10.1 2.7 %scatter_custom_fusion = bf16[450,1024]{0,1:T(8,128)(2,1)S(1)} fusion(s32[512]{0:T(512)S(1)} %bitcast.74, bf16[512,450]{1,0:T(8,128)(2,1)S(1)} %copy.20, bf16[]{:T(256)} %constant.18.clone.1), kind=kCustom, calls=%fused_computation.7 | custom fusion | bytes 921602 | tf_op jit(solution)/shard_map/scatter | solution.py:57
  12.8 0.1 constant_dynamic-slice_fusion
  12.9 0.1 copy.28
  13.1 0.1 copy.27
  13.2 0.1 copy.26
  13.4 0.1 copy.25
  13.5 0.1 copy.24
  13.7 0.1 copy.23
  13.8 0.1 copy.22
  14.0 0.1 copy.21
  14.1 0.6 %collective-permute-start.2 = (bf16[450,128]{1,0:T(8,128)(2,1)S(1)}, bf16[450,128]{1,0:T(8,128)(2,1)S(1)}, u32[]{:S(2)}, u32[]{:S(2)}) collective-permute-start(bf16[450,128]{1,0:T(8,128)(2,1)S(1)} %bitcast.70), channel_id=1, source_target_pairs={{0,1},{1,0},{2,3},{3,2},{4,5},{5,4},{6,7},{7,6},{8,9},{9,8},{10,11... | collective-permute-start | bytes 345608 | tf_op jit(solution)/shard_map/ppermute | solution.py:64
  14.7 3.9 %collective-permute-start.3 = (bf16[450,128]{1,0:T(8,128)(2,1)S(1)}, bf16[450,128]{1,0:T(8,128)(2,1)S(1)}, u32[]{:S(2)}, u32[]{:S(2)}) collective-permute-start(bf16[450,128]{1,0:T(8,128)(2,1)S(1)} %bitcast.69), channel_id=1, source_target_pairs={{0,2},{1,3},{2,0},{3,1},{4,6},{5,7},{6,4},{7,5},{8,10},{9,11},{10,... | collective-permute-start | bytes 345608 | tf_op jit(solution)/shard_map/ppermute | solution.py:64
  18.6 0.3 collective-permute-start.4
  19.0 0.2 collective-permute-start.5
  19.2 2.7 %collective-permute-start.6 = (bf16[450,128]{1,0:T(8,128)(2,1)S(1)}, bf16[450,128]{1,0:T(8,128)(2,1)S(1)}, u32[]{:S(2)}, u32[]{:S(2)}) collective-permute-start(bf16[450,128]{1,0:T(8,128)(2,1)S(1)} %bitcast.66), channel_id=1, source_target_pairs={{0,5},{1,4},{2,7},{3,6},{4,1},{5,0},{6,3},{7,2},{8,13},{9,12},{10,... | collective-permute-start | bytes 345608 | tf_op jit(solution)/shard_map/ppermute | solution.py:64
  21.9 0.0 collective-permute-done.2
  21.9 0.1 collective-permute-start.7
  22.0 0.0 collective-permute-done.3
  22.0 1.6 %collective-permute-start.8 = (bf16[450,128]{1,0:T(8,128)(2,1)S(1)}, bf16[450,128]{1,0:T(8,128)(2,1)S(1)}, u32[]{:S(2)}, u32[]{:S(2)}) collective-permute-start(bf16[450,128]{1,0:T(8,128)(2,1)S(1)} %bitcast.64), channel_id=1, source_target_pairs={{0,7},{1,6},{2,5},{3,4},{4,3},{5,2},{6,1},{7,0},{8,15},{9,14},{10,... | collective-permute-start | bytes 345608 | tf_op jit(solution)/shard_map/ppermute | solution.py:64
  23.6 1.7 %collective-permute-done.4 = bf16[450,128]{1,0:T(8,128)(2,1)S(1)} collective-permute-done((bf16[450,128]{1,0:T(8,128)(2,1)S(1)}, bf16[450,128]{1,0:T(8,128)(2,1)S(1)}, u32[]{:S(2)}, u32[]{:S(2)}) %collective-permute-start.4) | collective-permute-done | bytes 115232 | tf_op jit(solution)/shard_map/ppermute | solution.py:64
  25.3 0.7 %collective-permute-done.5 = bf16[450,128]{1,0:T(8,128)(2,1)S(1)} collective-permute-done((bf16[450,128]{1,0:T(8,128)(2,1)S(1)}, bf16[450,128]{1,0:T(8,128)(2,1)S(1)}, u32[]{:S(2)}, u32[]{:S(2)}) %collective-permute-start.5) | collective-permute-done | bytes 115232 | tf_op jit(solution)/shard_map/ppermute | solution.py:64
  26.0 8.8 %collective-permute-done.6 = bf16[450,128]{1,0:T(8,128)(2,1)S(1)} collective-permute-done((bf16[450,128]{1,0:T(8,128)(2,1)S(1)}, bf16[450,128]{1,0:T(8,128)(2,1)S(1)}, u32[]{:S(2)}, u32[]{:S(2)}) %collective-permute-start.6) | collective-permute-done | bytes 115232 | tf_op jit(solution)/shard_map/ppermute | solution.py:64
  34.9 5.5 %collective-permute-done.7 = bf16[450,128]{1,0:T(8,128)(2,1)S(1)} collective-permute-done((bf16[450,128]{1,0:T(8,128)(2,1)S(1)}, bf16[450,128]{1,0:T(8,128)(2,1)S(1)}, u32[]{:S(2)}, u32[]{:S(2)}) %collective-permute-start.7) | collective-permute-done | bytes 115232 | tf_op jit(solution)/shard_map/ppermute | solution.py:64
  40.4 2.5 %collective-permute-done.8 = bf16[450,128]{1,0:T(8,128)(2,1)S(1)} collective-permute-done((bf16[450,128]{1,0:T(8,128)(2,1)S(1)}, bf16[450,128]{1,0:T(8,128)(2,1)S(1)}, u32[]{:S(2)}, u32[]{:S(2)}) %collective-permute-start.8) | collective-permute-done | bytes 115232 | tf_op jit(solution)/shard_map/ppermute | solution.py:64
  42.9 0.7 %gather_fusion.1 = bf16[8,450,128]{2,1,0:T(8,128)(2,1)S(1)} fusion(bf16[8,450,128]{2,1,0:T(8,128)(2,1)S(1)} %bitcast_dynamic-update-slice_fusion, s32[1024]{0:T(1024)S(1)} %pad_clamp_fusion), kind=kCustom, calls=%fused_computation.1 | custom fusion | bytes 1843232 | tf_op jit(solution)/shard_map/gather | solution.py:65
  43.6 0.1 copy.29
  43.8 0.4 reshape_reshape.3
  44.2 0.0 copy-done
  44.2 3.2 %convert_bitcast_fusion = bf16[5,400,1024]{2,1,0:T(8,128)(2,1)} fusion(bf16[5,90,1024]{2,1,0:T(8,128)(2,1)S(1)} %reshape_reshape.3, bf16[5,400,90]{1,2,0:T(8,128)(2,1)S(1)} %copy-done), kind=kOutput, calls=%fused_computation.3 | convolution fusion | flops 370688000 | bytes 5377600 | tf_op jit(solution)/shard_map/vcl,vln->vcn/dot_general | solution.py:33
  (14 shorter events, 0.2 us)
Async XLA Ops:
  0.0 44.2 %copy-start = (bf16[5,400,90]{1,2,0:T(8,128)(2,1)S(1)}, bf16[5,400,90]{1,2,0:T(8,128)(2,1)}, u32[]{:S(2)}) copy-start(bf16[5,400,90]{1,2,0:T(8,128)(2,1)} %param.9) | copy-start | bytes 1080004
  0.0 6.3 %collective-permute-start = (bf16[1,450,128]{2,1,0:T(8,128)(2,1)}, bf16[1,450,128]{2,1,0:T(8,128)(2,1)S(1)}, u32[]{:S(2)}, u32[]{:S(2)}) collective-permute-start(bf16[1,450,128]{2,1,0:T(8,128)(2,1)} %param.5), channel_id=1, source_target_pairs={{0,1},{1,2},{2,3},{3,4},{4,5},{5,6},{6,7},{7,8},{8,9},{9,10},{10,1... | collective-permute-start | bytes 345608 | tf_op jit(solution)/shard_map/ppermute | solution.py:25
  1.9 4.5 %collective-permute-start.1 = (bf16[1,450,128]{2,1,0:T(8,128)(2,1)}, bf16[1,450,128]{2,1,0:T(8,128)(2,1)S(1)}, u32[]{:S(2)}, u32[]{:S(2)}) collective-permute-start(bf16[1,450,128]{2,1,0:T(8,128)(2,1)} %param.5), channel_id=1, source_target_pairs={{1,0},{2,1},{3,2},{4,3},{5,4},{6,5},{7,6},{8,7},{9,8},{10,9},{11,1... | collective-permute-start | bytes 345608 | tf_op jit(solution)/shard_map/ppermute | solution.py:26
  14.1 7.8 %collective-permute-start.2 = (bf16[450,128]{1,0:T(8,128)(2,1)S(1)}, bf16[450,128]{1,0:T(8,128)(2,1)S(1)}, u32[]{:S(2)}, u32[]{:S(2)}) collective-permute-start(bf16[450,128]{1,0:T(8,128)(2,1)S(1)} %bitcast.70), channel_id=1, source_target_pairs={{0,1},{1,0},{2,3},{3,2},{4,5},{5,4},{6,7},{7,6},{8,9},{9,8},{10,11... | collective-permute-start | bytes 345608 | tf_op jit(solution)/shard_map/ppermute | solution.py:64
  14.7 7.3 %collective-permute-start.3 = (bf16[450,128]{1,0:T(8,128)(2,1)S(1)}, bf16[450,128]{1,0:T(8,128)(2,1)S(1)}, u32[]{:S(2)}, u32[]{:S(2)}) collective-permute-start(bf16[450,128]{1,0:T(8,128)(2,1)S(1)} %bitcast.69), channel_id=1, source_target_pairs={{0,2},{1,3},{2,0},{3,1},{4,6},{5,7},{6,4},{7,5},{8,10},{9,11},{10,... | collective-permute-start | bytes 345608 | tf_op jit(solution)/shard_map/ppermute | solution.py:64
  18.6 6.6 %collective-permute-start.4 = (bf16[450,128]{1,0:T(8,128)(2,1)S(1)}, bf16[450,128]{1,0:T(8,128)(2,1)S(1)}, u32[]{:S(2)}, u32[]{:S(2)}) collective-permute-start(bf16[450,128]{1,0:T(8,128)(2,1)S(1)} %bitcast.68), channel_id=1, source_target_pairs={{0,3},{1,2},{2,1},{3,0},{4,7},{5,6},{6,5},{7,4},{8,11},{9,10},{10,... | collective-permute-start | bytes 345608 | tf_op jit(solution)/shard_map/ppermute | solution.py:64
  19.0 7.0 %collective-permute-start.5 = (bf16[450,128]{1,0:T(8,128)(2,1)S(1)}, bf16[450,128]{1,0:T(8,128)(2,1)S(1)}, u32[]{:S(2)}, u32[]{:S(2)}) collective-permute-start(bf16[450,128]{1,0:T(8,128)(2,1)S(1)} %bitcast.67), channel_id=1, source_target_pairs={{0,4},{1,5},{2,6},{3,7},{4,0},{5,1},{6,2},{7,3},{8,12},{9,13},{10,... | collective-permute-start | bytes 345608 | tf_op jit(solution)/shard_map/ppermute | solution.py:64
  19.2 15.7 %collective-permute-start.6 = (bf16[450,128]{1,0:T(8,128)(2,1)S(1)}, bf16[450,128]{1,0:T(8,128)(2,1)S(1)}, u32[]{:S(2)}, u32[]{:S(2)}) collective-permute-start(bf16[450,128]{1,0:T(8,128)(2,1)S(1)} %bitcast.66), channel_id=1, source_target_pairs={{0,5},{1,4},{2,7},{3,6},{4,1},{5,0},{6,3},{7,2},{8,13},{9,12},{10,... | collective-permute-start | bytes 345608 | tf_op jit(solution)/shard_map/ppermute | solution.py:64
  21.9 18.5 %collective-permute-start.7 = (bf16[450,128]{1,0:T(8,128)(2,1)S(1)}, bf16[450,128]{1,0:T(8,128)(2,1)S(1)}, u32[]{:S(2)}, u32[]{:S(2)}) collective-permute-start(bf16[450,128]{1,0:T(8,128)(2,1)S(1)} %bitcast.65), channel_id=1, source_target_pairs={{0,6},{1,7},{2,4},{3,5},{4,2},{5,3},{6,0},{7,1},{8,14},{9,15},{10,... | collective-permute-start | bytes 345608 | tf_op jit(solution)/shard_map/ppermute | solution.py:64
  22.0 20.9 %collective-permute-start.8 = (bf16[450,128]{1,0:T(8,128)(2,1)S(1)}, bf16[450,128]{1,0:T(8,128)(2,1)S(1)}, u32[]{:S(2)}, u32[]{:S(2)}) collective-permute-start(bf16[450,128]{1,0:T(8,128)(2,1)S(1)} %bitcast.64), channel_id=1, source_target_pairs={{0,7},{1,6},{2,5},{3,4},{4,3},{5,2},{6,1},{7,0},{8,15},{9,14},{10,... | collective-permute-start | bytes 345608 | tf_op jit(solution)/shard_map/ppermute | solution.py:64
